TPU v7x, 32 devices: a whole 2x2x4 slice. The times are simulated.
32 devices in a mesh: wide: 8 (over z, x), narrow: 4 (over y, core).
Axes of the slice: x: 2, y: 2, z: 4, core: 2. Of those that a mesh axis runs over, the one named last changes fastest.
Arguments:
- points: bfloat16 [32768, 256], P('wide'), may hold values from -6 to 6
- q_init: float32 [16, 32768], P(None, 'wide'), may hold values from -80 to 80
- pairs: int32 [2, 2048], P(None, ('wide', 'narrow')), may hold values from 0 to 255, as said below
Outputs:
- basis: float32 [16, 32768], P(None, 'wide')
- coeffs: float32 [3, 2, 16, 16], replicated
Inputs may be any that keep to these rules, and one draw needn't show every extreme that they name: `pairs`: pair number g * 4 * 64 + m * 64 + o * 8 + c (g < 8, m < 4, o < 8, c < 8) has its first block in g * 32 .. (g + 1) * 32 - 1 and its second block in o * 32 .. (o + 1) * 32 - 1; the two ends of a pair differ.
All inputs are finite; a program needn't handle non-finite values.
Results may differ from a plain program's by a relative error of at most 0.0015.
Values may be sent and summed in bfloat16 or wider, within the bound.
A program may use at most 64 MiB of HBM per device.

v0:
```python
import jax
import jax.numpy as jnp
from jax import lax
from jax.sharding import PartitionSpec as P

BS = 128
STEPS = 3
KERNEL_FACTOR = 3.0
EPSILON = 1e-06
HIGH = lax.Precision.HIGHEST
pair_group = 32


def unit_rows(points):
    wide32 = points.astype(jnp.float32)
    scaled = wide32 * lax.rsqrt(jnp.sum(wide32 * wide32, axis=-1, keepdims=True) + EPSILON)
    return scaled.astype(jnp.bfloat16)


def tile_terms(first_pts, second_pts, first_vec, second_vec):
    inner_products = jnp.einsum(
        "paf,pbf->pab", first_pts, second_pts, preferred_element_type=jnp.float32
    )
    kernel_values = jnp.exp(KERNEL_FACTOR * (inner_products - 1.0))
    to_first = jnp.einsum("pab,prb->pra", kernel_values, second_vec, precision=HIGH)
    to_second = jnp.einsum("pab,pra->prb", kernel_values, first_vec, precision=HIGH)
    return (to_first, to_second)


def per_device(points, q_init, pairs):
    wide_count = lax.axis_size("wide")
    wide_pos = lax.axis_index("wide")
    own_blocks = points.shape[0] // BS
    width = points.shape[1]
    vec_rows = q_init.shape[0]
    pair_count = pairs.shape[1]
    capacity = pair_count // wide_count
    total_points = own_blocks * BS * wide_count
    unit = unit_rows(points).reshape(own_blocks, BS, width)
    first_local = pairs[0] - wide_pos * own_blocks
    wanted = pairs[1].reshape(wide_count, capacity)
    local_ids = (
        lax.all_to_all(wanted, "wide", split_axis=0, concat_axis=0, tiled=True)
        - wide_pos * own_blocks
    )
    replies = lax.all_to_all(unit[local_ids], "wide", split_axis=0, concat_axis=0, tiled=True)
    second_pts = replies
    second_pts = second_pts.reshape(pair_count, BS, width)
    targets = jnp.concatenate([first_local, local_ids.reshape(pair_count)], axis=0)
    owners = (jnp.arange(own_blocks, dtype=jnp.int32)[:, None] == targets[None, :]).astype(
        jnp.float32
    )

    def grouped(values):
        return values.reshape((pair_count // pair_group, pair_group) + values.shape[1:])

    def single_group(items):
        first_ids, second_p, first_v, second_v = items
        return tile_terms(unit[first_ids], second_p, first_v, second_v)

    def gram_sums(values):
        return lax.psum(values, "wide")

    gram0 = gram_sums(jnp.dot(q_init, q_init.T, precision=HIGH)) / total_points
    factor0 = jnp.linalg.cholesky(gram0)
    present_portion = lax.linalg.triangular_solve(factor0, q_init, left_side=True, lower=True)
    current = present_portion
    previous = jnp.zeros_like(present_portion)
    last = jnp.zeros((vec_rows, vec_rows), jnp.float32)
    records = []
    for step in range(STEPS):
        rows = current.reshape(vec_rows, own_blocks, BS).transpose(1, 0, 2)
        second_vec = lax.all_to_all(
            rows[local_ids], "wide", split_axis=0, concat_axis=0, tiled=True
        ).reshape(pair_count, vec_rows, BS)
        first_vec = rows[first_local]
        to_first, to_second = lax.map(
            single_group,
            (grouped(first_local), grouped(second_pts), grouped(first_vec), grouped(second_vec)),
        )
        to_first = to_first.reshape(pair_count, vec_rows * BS)
        returned = lax.all_to_all(
            to_second.reshape(wide_count, capacity, vec_rows * BS),
            "wide",
            split_axis=0,
            concat_axis=0,
            tiled=True,
        )
        terms = jnp.concatenate([to_first, returned.reshape(pair_count, vec_rows * BS)], axis=0)
        summed_blocks = jnp.dot(owners, terms, precision=HIGH)
        summed_blocks = lax.psum(summed_blocks, "narrow")
        image = summed_blocks.reshape(-1, vec_rows, BS).transpose(1, 0, 2).reshape(vec_rows, -1)
        residual = image - jnp.dot(last.T, previous, precision=HIGH)
        raw, cross, basis_gram = gram_sums(
            (
                jnp.dot(residual, residual.T, precision=HIGH),
                jnp.dot(present_portion, residual.T, precision=HIGH),
                jnp.dot(present_portion, present_portion.T, precision=HIGH),
            )
        )
        along = cross / total_points
        raw = raw / total_points
        basis_gram = basis_gram / total_points
        remainder = residual - jnp.dot(along.T, present_portion, precision=HIGH)
        squared = jnp.dot(along.T, along, precision=HIGH)
        gram = (
            raw
            - 2.0 * squared
            + jnp.dot(along.T, jnp.dot(basis_gram, along, precision=HIGH), precision=HIGH)
        )
        factor = jnp.linalg.cholesky(gram)
        records.append(jnp.stack([along, factor]))
        previous = present_portion
        last = factor
        present_portion = lax.linalg.triangular_solve(factor, remainder, left_side=True, lower=True)
        current = present_portion
    return (current, jnp.stack(records))


def solution(mesh):
    placed = (P("wide", None), P(None, "wide"), P(None, ("wide", "narrow")))
    return jax.shard_map(
        per_device, mesh=mesh, in_specs=placed, out_specs=(P(None, "wide"), P()), check_vma=False
    )
```

profile of v0, /device:TPU:0, one launch (start us, length us, event | category | flops | bytes accessed | tf_op | source)
XLA Modules:
  0.0 559.8 jit_solution(13503507722654973966)
XLA Ops:
  8.6 7.3 %all-to-all-start = ((s32[8,1,8]{2,1,0:T(1,128)}), s32[8,1,8]{2,1,0:T(1,128)S(1)}, u32[]{:S(2)}, u32[]{:S(2)}) async-start(s32[8,1,8]{2,1,0:T(1,128)} %bitcast.22), calls=%async_computation | async-start | bytes 8192 | tf_op jit(solution)/shard_map/all_to_all | solution.py:43
  16.4 22.1 %psum.91 = f32[16,16]{1,0:T(8,128)S(1)} all-reduce(f32[16,16]{1,0:T(8,128)S(1)} %fusion.187), channel_id=1, replica_groups=mesh['wide'=8,'narrow'=4] {'wide'}, use_global_device_ids=true, to_apply=%region_1.0 | all-reduce | flops 256 | bytes 2048 | tf_op jit(solution)/shard_map/psum | solution.py:62
  46.9 3.5 all-to-all-start.1
  55.1 5.6 %all-to-all-done.1 = f32[8,8,16,128]{3,2,1,0:T(8,128)S(1)} async-done(((f32[8,8,16,128]{3,2,1,0:T(8,128)}), f32[8,8,16,128]{3,2,1,0:T(8,128)S(1)}, u32[]{:S(2)}, u32[]{:S(2)}) %all-to-all-start.1) | async-done | bytes 524320 | tf_op jit(solution)/shard_map/all_to_all | solution.py:73
  60.7 4.7 all-to-all-start.2
  67.0 87.2 %all-to-all-done.2 = bf16[8,8,128,256]{3,2,1,0:T(8,128)(2,1)} async-done(((bf16[8,8,128,256]{3,2,1,0:T(8,128)(2,1)}), bf16[8,8,128,256]{3,2,1,0:T(8,128)(2,1)}, u32[]{:S(2)}, u32[]{:S(2)}) %all-to-all-start.2) | async-done | bytes 4194336 | tf_op jit(solution)/shard_map/all_to_all | solution.py:46
  155.9 23.6 %while.42 = (s32[]{:T(128)}, f32[2,32,16,128]{3,2,1,0:T(8,128)}, f32[2,32,16,128]{3,2,1,0:T(8,128)}, f32[2,32,16,128]{3,2,1,0:T(8,128)S(1)}, s32[2,32]{1,0:T(2,1...) while((s32[]{:T(128)}, f32[2,32,16,128]{3,2,1,0:T(8,128)}, ...), condition=%wide.region_5.8_spmd, body=%wide.region_4.7_spmd.sunk | while | flops 471860320 | bytes 17833084 | solution.py:77
  160.9 4.1 fusion.265
  172.7 4.1 fusion.265
  181.5 3.5 all-to-all-start.3
  187.2 12.4 %all-to-all-done.3 = f32[8,8,2048]{2,1,0:T(8,128)S(1)} async-done(((f32[8,8,2048]{2,1,0:T(8,128)}), f32[8,8,2048]{2,1,0:T(8,128)S(1)}, u32[]{:S(2)}, u32[]{:S(2)}) %all-to-all-start.3) | async-done | bytes 524320 | tf_op jit(solution)/shard_map/all_to_all | solution.py:82
  202.4 31.1 %all-reduce.7.cloned.1.call-done = f32[16,4096]{1,0:T(8,128)} async-done(((f32[16,4096]{1,0:T(8,128)}), f32[16,4096]{1,0:T(8,128)}) %all-reduce.7.cloned.1.call-update) | async-done | bytes 262160 | tf_op jit(solution)/shard_map/psum | solution.py:91
  235.6 37.1 %all-reduce.2 = (f32[16,16]{1,0:T(8,128)S(1)}, f32[16,16]{1,0:T(8,128)S(1)}, f32[16,16]{1,0:T(8,128)S(1)}) all-reduce(f32[16,16]{1,0:T(8,128)S(1)} %fusion.189, f32[16,16]{1,0:T(8,128)S(1)} %fusion.188, f32[16,16]{1,0:T(8,128)S(1)} %fusion.190), channel_id=1, replica_groups=mesh['wide'=8,'narrow'=4] {'wide'}, use_global_device_ids=true, to_apply=%region_8.11 | all-reduce | flops 768 | bytes 6144 | tf_op jit(solution)/shard_map/psum | solution.py:62
  279.7 4.1 all-to-all-start.4
  285.3 8.8 %all-to-all-done.4 = f32[8,8,16,128]{3,2,1,0:T(8,128)} async-done(((f32[8,8,16,128]{3,2,1,0:T(8,128)}), f32[8,8,16,128]{3,2,1,0:T(8,128)}, u32[]{:S(2)}, u32[]{:S(2)}) %all-to-all-start.4) | async-done | bytes 524320 | tf_op jit(solution)/shard_map/all_to_all | solution.py:73
  295.8 25.6 %while.43 = (s32[]{:T(128)}, f32[2,32,16,128]{3,2,1,0:T(8,128)}, f32[2,32,16,128]{3,2,1,0:T(8,128)}, f32[2,32,16,128]{3,2,1,0:T(8,128)}, s32[2,32]{1,0:T(2,128)S...) while((s32[]{:T(128)}, f32[2,32,16,128]{3,2,1,0:T(8,128)}, ...), condition=%wide.region_11.14_spmd, body=%wide.region_10.13_spmd.sunk | while | flops 471860320 | bytes 17833084 | solution.py:77
  297.8 2.9 fusion.272
  300.7 5.1 fusion.273
  313.5 5.1 fusion.273
  323.2 3.7 all-to-all-start.5
  329.0 8.2 %all-to-all-done.5 = f32[8,8,2048]{2,1,0:T(8,128)S(1)} async-done(((f32[8,8,2048]{2,1,0:T(8,128)}), f32[8,8,2048]{2,1,0:T(8,128)S(1)}, u32[]{:S(2)}, u32[]{:S(2)}) %all-to-all-start.5) | async-done | bytes 524320 | tf_op jit(solution)/shard_map/all_to_all | solution.py:82
  339.9 30.2 %all-reduce.9.cloned.1.call-done = f32[16,4096]{1,0:T(8,128)} async-done(((f32[16,4096]{1,0:T(8,128)}), f32[16,4096]{1,0:T(8,128)}) %all-reduce.9.cloned.1.call-update) | async-done | bytes 262160 | tf_op jit(solution)/shard_map/psum | solution.py:91
  373.0 37.1 %all-reduce.1 = (f32[16,16]{1,0:T(8,128)S(1)}, f32[16,16]{1,0:T(8,128)S(1)}, f32[16,16]{1,0:T(8,128)S(1)}) all-reduce(f32[16,16]{1,0:T(8,128)S(1)} %fusion.192, f32[16,16]{1,0:T(8,128)S(1)} %fusion.191, f32[16,16]{1,0:T(8,128)S(1)} %fusion.193), channel_id=1, replica_groups=mesh['wide'=8,'narrow'=4] {'wide'}, use_global_device_ids=true, to_apply=%region_14.17 | all-reduce | flops 768 | bytes 6144 | tf_op jit(solution)/shard_map/psum | solution.py:62
  417.0 4.4 all-to-all-start.6
  422.8 8.6 %all-to-all-done.6 = f32[8,8,16,128]{3,2,1,0:T(8,128)} async-done(((f32[8,8,16,128]{3,2,1,0:T(8,128)}), f32[8,8,16,128]{3,2,1,0:T(8,128)}, u32[]{:S(2)}, u32[]{:S(2)}) %all-to-all-start.6) | async-done | bytes 524320 | tf_op jit(solution)/shard_map/all_to_all | solution.py:73
  433.1 25.6 %while.44 = (s32[]{:T(128)}, f32[2,32,16,128]{3,2,1,0:T(8,128)}, f32[2,32,16,128]{3,2,1,0:T(8,128)}, f32[2,32,16,128]{3,2,1,0:T(8,128)}, s32[2,32]{1,0:T(2,128)S...) while((s32[]{:T(128)}, f32[2,32,16,128]{3,2,1,0:T(8,128)}, ...), condition=%wide.region_17.20_spmd, body=%wide.region_16.19_spmd.sunk | while | flops 471860320 | bytes 17833084 | solution.py:77
  438.0 5.1 fusion.281
  450.8 5.1 fusion.281
  460.6 3.7 all-to-all-start.7
  466.0 8.5 %all-to-all-done.7 = f32[8,8,2048]{2,1,0:T(8,128)S(1)} async-done(((f32[8,8,2048]{2,1,0:T(8,128)}), f32[8,8,2048]{2,1,0:T(8,128)S(1)}, u32[]{:S(2)}, u32[]{:S(2)}) %all-to-all-start.7) | async-done | bytes 524320 | tf_op jit(solution)/shard_map/all_to_all | solution.py:82
  475.8 30.6 %all-reduce.11.cloned.1.call-done = f32[16,4096]{1,0:T(8,128)} async-done(((f32[16,4096]{1,0:T(8,128)}), f32[16,4096]{1,0:T(8,128)}) %all-reduce.11.cloned.1.call-update) | async-done | bytes 262160 | tf_op jit(solution)/shard_map/psum | solution.py:91
  509.3 37.1 %all-reduce = (f32[16,16]{1,0:T(8,128)S(1)}, f32[16,16]{1,0:T(8,128)S(1)}, f32[16,16]{1,0:T(8,128)S(1)}) all-reduce(f32[16,16]{1,0:T(8,128)S(1)} %fusion.195, f32[16,16]{1,0:T(8,128)S(1)} %fusion.194, f32[16,16]{1,0:T(8,128)S(1)} %fusion.196), channel_id=1, replica_groups=mesh['wide'=8,'narrow'=4] {'wide'}, use_global_device_ids=true, to_apply=%region_20.23 | all-reduce | flops 768 | bytes 6144 | tf_op jit(solution)/shard_map/psum | solution.py:62
  (163 shorter events, 114.8 us)
Async XLA Ops:
  7.2 8.8 %copy-start = (f32[16,4096]{1,0:T(8,128)S(1)}, f32[16,4096]{1,0:T(8,128)}, u32[]{:S(2)}) copy-start(f32[16,4096]{1,0:T(8,128)} %param.13) | copy-start | bytes 786436
  8.6 36.7 %all-to-all-start = ((s32[8,1,8]{2,1,0:T(1,128)}), s32[8,1,8]{2,1,0:T(1,128)S(1)}, u32[]{:S(2)}, u32[]{:S(2)}) async-start(s32[8,1,8]{2,1,0:T(1,128)} %bitcast.22), calls=%async_computation | async-start | bytes 8192 | tf_op jit(solution)/shard_map/all_to_all | solution.py:43
  46.9 13.9 %all-to-all-start.1 = ((f32[8,8,16,128]{3,2,1,0:T(8,128)}), f32[8,8,16,128]{3,2,1,0:T(8,128)S(1)}, u32[]{:S(2)}, u32[]{:S(2)}) async-start(f32[8,8,16,128]{3,2,1,0:T(8,128)} %bitcast.29), calls=%async_computation.1 | async-start | bytes 1048576 | tf_op jit(solution)/shard_map/all_to_all | solution.py:73
  60.7 4.7 copy-start.4
  60.7 93.5 %all-to-all-start.2 = ((bf16[8,8,128,256]{3,2,1,0:T(8,128)(2,1)}), bf16[8,8,128,256]{3,2,1,0:T(8,128)(2,1)}, u32[]{:S(2)}, u32[]{:S(2)}) async-start(bf16[8,8,128,256]{3,2,1,0:T(8,128)(2,1)} %bitcast.312), calls=%async_computation.2 | async-start | bytes 8388608 | tf_op jit(solution)/shard_map/all_to_all | solution.py:46
  160.9 4.1 copy-start.2
  172.7 4.1 copy-start.2
  181.5 18.2 %all-to-all-start.3 = ((f32[8,8,2048]{2,1,0:T(8,128)}), f32[8,8,2048]{2,1,0:T(8,128)S(1)}, u32[]{:S(2)}, u32[]{:S(2)}) async-start(f32[8,8,2048]{2,1,0:T(8,128)} %reshape.254), calls=%async_computation.3 | async-start | bytes 1048576 | tf_op jit(solution)/shard_map/all_to_all | solution.py:82
  185.0 48.6 %all-reduce.7.cloned.1.call-start = ((), (), s32[]{:S(2)}) async-start(), calls=%async_computation.8 | async-start | bytes 524288 | tf_op jit(solution)/shard_map/psum | solution.py:91
  279.7 14.4 %all-to-all-start.4 = ((f32[8,8,16,128]{3,2,1,0:T(8,128)}), f32[8,8,16,128]{3,2,1,0:T(8,128)}, u32[]{:S(2)}, u32[]{:S(2)}) async-start(f32[8,8,16,128]{3,2,1,0:T(8,128)} %bitcast.324), calls=%async_computation.4 | async-start | bytes 1048576 | tf_op jit(solution)/shard_map/all_to_all | solution.py:73
  300.7 5.1 copy-start.3
  313.5 5.1 copy-start.3
  323.2 13.9 %all-to-all-start.5 = ((f32[8,8,2048]{2,1,0:T(8,128)}), f32[8,8,2048]{2,1,0:T(8,128)S(1)}, u32[]{:S(2)}, u32[]{:S(2)}) async-start(f32[8,8,2048]{2,1,0:T(8,128)} %reshape.261), calls=%async_computation.5 | async-start | bytes 1048576 | tf_op jit(solution)/shard_map/all_to_all | solution.py:82
  326.9 43.2 %all-reduce.9.cloned.1.call-start = ((), (), s32[]{:S(2)}) async-start(), calls=%async_computation.9 | async-start | bytes 524288 | tf_op jit(solution)/shard_map/psum | solution.py:91
  417.0 14.4 %all-to-all-start.6 = ((f32[8,8,16,128]{3,2,1,0:T(8,128)}), f32[8,8,16,128]{3,2,1,0:T(8,128)}, u32[]{:S(2)}, u32[]{:S(2)}) async-start(f32[8,8,16,128]{3,2,1,0:T(8,128)} %bitcast.323), calls=%async_computation.6 | async-start | bytes 1048576 | tf_op jit(solution)/shard_map/all_to_all | solution.py:73
  438.0 5.1 copy-start.1
  450.8 5.1 copy-start.1
  460.6 13.9 %all-to-all-start.7 = ((f32[8,8,2048]{2,1,0:T(8,128)}), f32[8,8,2048]{2,1,0:T(8,128)S(1)}, u32[]{:S(2)}, u32[]{:S(2)}) async-start(f32[8,8,2048]{2,1,0:T(8,128)} %reshape.268), calls=%async_computation.7 | async-start | bytes 1048576 | tf_op jit(solution)/shard_map/all_to_all | solution.py:82
  464.2 42.2 %all-reduce.11.cloned.1.call-start = ((), (), s32[]{:S(2)}) async-start(), calls=%async_computation.10 | async-start | bytes 524288 | tf_op jit(solution)/shard_map/psum | solution.py:91
Sparse Core Ops, SparseCore 0:
  202.1 31.3 all-reduce.6
  339.6 30.4 all-reduce.8
  475.9 30.4 all-reduce.10
where the time goes:
time: 561 us; the launch traced here: 560 us
  waiting for transfers between devices  231 us (41%)
  blocking collectives  133 us (24%)
  matrix products  80.9 us (14%)
  local copies, waits for them, and re-layouts  43.4 us (8%)
  starting transfers between devices  34.9 us (6%)
  other arithmetic  21.7 us (4%)
  between operations  14.1 us (3%)
    psum x4, blocking collectives, gram_sums(): return lax.psum(values, 'wide')  133 us
    psum x3, waiting for transfers between devices, per_device(): summed_blocks = lax.psum(summed_blocks, 'narrow')  91.8 us
    all_to_all x1, waiting for transfers between devices, per_device(): lax.all_to_all(unit[local_ids], 'wide', split_axis=0, concat_axis=0, tile...  87.2 us
    all_to_all x3, waiting for transfers between devices, per_device(): lax.all_to_all(to_second.reshape(wide_count, capacity, vec_rows * BS), 'w...  29.2 us
    dot_general x6, matrix products, tile_terms(): jnp.einsum('pab,prb->pra', kernel_values, second_vec, precision=HIGH)  28.5 us
    all_to_all x3, waiting for transfers between devices, per_device(): lax.all_to_all(rows[local_ids], 'wide', split_axis=0, concat_axis=0, tile...  23.1 us
    dot_general x6, matrix products, tile_terms(): jnp.einsum('paf,pbf->pab', first_pts, second_pts, preferred_element_type=...  17.6 us
    dot_general x6, matrix products, tile_terms(): jnp.einsum('pab,pra->prb', kernel_values, first_vec, precision=HIGH)  16.5 us
  transfers between devices with their start and end apart: 11, of which 10 were waited for; matrix products, arithmetic and copies ran while one was open for 4% of the time, Pallas kernels for 0%

commit v1 on v0

--- a/solution.py
+++ b/solution.py
@@ -9,6 +9,20 @@
 EPSILON = 1e-06
 HIGH = lax.Precision.HIGHEST
 pair_group = 32
+
+
+def _close_lines(x0):
+    axis_id = "narrow"
+    k_all = lax.axis_size(axis_id)
+
+    def body_change(v1, z1):
+        if z1 >= k_all:
+            return v1
+        return body_change(
+            v1 + lax.ppermute(v1, axis_id, [(m, m ^ z1) for m in range(k_all)]), 2 * z1
+        )
+
+    return body_change(x0, 1)
 
 
 def unit_rows(points):
@@ -88,7 +102,7 @@
         )
         terms = jnp.concatenate([to_first, returned.reshape(pair_count, vec_rows * BS)], axis=0)
         summed_blocks = jnp.dot(owners, terms, precision=HIGH)
-        summed_blocks = lax.psum(summed_blocks, "narrow")
+        summed_blocks = _close_lines(summed_blocks)
         image = summed_blocks.reshape(-1, vec_rows, BS).transpose(1, 0, 2).reshape(vec_rows, -1)
         residual = image - jnp.dot(last.T, previous, precision=HIGH)
         raw, cross, basis_gram = gram_sums(

time: 561 us -> 475 us (0.85)
  waiting for transfers between devices: 231 us -> 164 us
  between operations: 14.1 us -> 1.05 us
    psum x3 -> x0, waiting for transfers between devices: 91.8 us -> none  [per_device(): summed_blocks = lax.psum(summed_blocks, 'narrow')]
    ppermute x0 -> x6, waiting for transfers between devices: none -> 23.6 us  [body_change(): lax.ppermute(v1, axis_id, [(m, m ^ z1) for m in range(k_all)])]
  transfers between devices with their start and end apart: 11 -> 14, of which waited for: 10 -> 13; matrix products, arithmetic and copies ran while one was open for 4% -> 5% of each run, Pallas kernels for 0% -> 0%
where the time goes in v1:
time: 475 us; the launch traced here: 474 us
  waiting for transfers between devices  164 us (35%)
  blocking collectives  128 us (27%)
  matrix products  78.2 us (16%)
  local copies, waits for them, and re-layouts  41.2 us (9%)
  starting transfers between devices  39.8 us (8%)
  other arithmetic  22.1 us (5%)
    psum x4, blocking collectives, gram_sums(): return lax.psum(values, 'wide')  128 us
    all_to_all x1, waiting for transfers between devices, per_device(): lax.all_to_all(unit[local_ids], 'wide', split_axis=0, concat_axis=0, tile...  87.2 us
    all_to_all x3, waiting for transfers between devices, per_device(): lax.all_to_all(to_second.reshape(wide_count, capacity, vec_rows * BS), 'w...  29.8 us
    dot_general x6, matrix products, tile_terms(): jnp.einsum('pab,prb->pra', kernel_values, second_vec, precision=HIGH)  28.5 us
    ppermute x6, waiting for transfers between devices, body_change(): lax.ppermute(v1, axis_id, [(m, m ^ z1) for m in range(k_all)])  23.6 us
    all_to_all x3, waiting for transfers between devices, per_device(): lax.all_to_all(rows[local_ids], 'wide', split_axis=0, concat_axis=0, tile...  23 us
    dot_general x6, matrix products, tile_terms(): jnp.einsum('paf,pbf->pab', first_pts, second_pts, preferred_element_type=...  17.6 us
    dot_general x6, matrix products, tile_terms(): jnp.einsum('pab,pra->prb', kernel_values, first_vec, precision=HIGH)  16.5 us
  transfers between devices with their start and end apart: 14, of which 13 were waited for; matrix products, arithmetic and copies ran while one was open for 5% of the time, Pallas kernels for 0%

profile of v1, /device:TPU:0, one launch (start us, length us, event | category | flops | bytes accessed | tf_op | source)
XLA Modules:
  0.0 473.9 jit_solution(223559767498268323)
XLA Ops:
  2.1 7.3 %all-to-all-start = ((s32[8,1,8]{2,1,0:T(1,128)}), s32[8,1,8]{2,1,0:T(1,128)S(1)}, u32[]{:S(2)}, u32[]{:S(2)}) async-start(s32[8,1,8]{2,1,0:T(1,128)} %bitcast.22), calls=%async_computation | async-start | bytes 8192 | tf_op jit(solution)/shard_map/all_to_all | solution.py:57
  9.8 22.1 %psum.70 = f32[16,16]{1,0:T(8,128)S(1)} all-reduce(f32[16,16]{1,0:T(8,128)S(1)} %fusion.190), channel_id=1, replica_groups=mesh['wide'=8,'narrow'=4] {'wide'}, use_global_device_ids=true, to_apply=%region_1.0 | all-reduce | flops 256 | bytes 2048 | tf_op jit(solution)/shard_map/psum | solution.py:76
  40.4 3.5 all-to-all-start.1
  48.6 5.6 %all-to-all-done.1 = f32[8,8,16,128]{3,2,1,0:T(8,128)S(1)} async-done(((f32[8,8,16,128]{3,2,1,0:T(8,128)}), f32[8,8,16,128]{3,2,1,0:T(8,128)S(1)}, u32[]{:S(2)}, u32[]{:S(2)}) %all-to-all-start.1) | async-done | bytes 524320 | tf_op jit(solution)/shard_map/all_to_all | solution.py:87
  54.2 4.7 all-to-all-start.2
  60.5 87.2 %all-to-all-done.2 = bf16[8,8,128,256]{3,2,1,0:T(8,128)(2,1)} async-done(((bf16[8,8,128,256]{3,2,1,0:T(8,128)(2,1)}), bf16[8,8,128,256]{3,2,1,0:T(8,128)(2,1)}, u32[]{:S(2)}, u32[]{:S(2)}) %all-to-all-start.2) | async-done | bytes 4194336 | tf_op jit(solution)/shard_map/all_to_all | solution.py:60
  149.4 23.6 %while.42 = (s32[]{:T(128)}, f32[2,32,16,128]{3,2,1,0:T(8,128)}, f32[2,32,16,128]{3,2,1,0:T(8,128)}, f32[2,32,16,128]{3,2,1,0:T(8,128)S(1)}, s32[2,32]{1,0:T(2,1...) while((s32[]{:T(128)}, f32[2,32,16,128]{3,2,1,0:T(8,128)}, ...), condition=%wide.region_5.8_spmd, body=%wide.region_4.7_spmd.sunk | while | flops 471860320 | bytes 17833084 | solution.py:91
  154.4 4.1 fusion.268
  166.2 4.1 fusion.268
  174.9 3.5 all-to-all-start.3
  180.6 12.5 %all-to-all-done.3 = f32[8,8,2048]{2,1,0:T(8,128)S(1)} async-done(((f32[8,8,2048]{2,1,0:T(8,128)}), f32[8,8,2048]{2,1,0:T(8,128)S(1)}, u32[]{:S(2)}, u32[]{:S(2)}) %all-to-all-start.3) | async-done | bytes 524320 | tf_op jit(solution)/shard_map/all_to_all | solution.py:96
  198.3 6.3 %collective-permute-done.1 = f32[32,2048]{1,0:T(8,128)S(1)} collective-permute-done((f32[32,2048]{1,0:T(8,128)S(1)}, f32[32,2048]{1,0:T(8,128)S(1)}, u32[]{:S(2)}, u32[]{:S(2)}) %collective-permute-start.1) | collective-permute-done | bytes 262176 | tf_op jit(solution)/shard_map/ppermute | solution.py:22
  205.9 35.2 %all-reduce.2 = (f32[16,16]{1,0:T(8,128)S(1)}, f32[16,16]{1,0:T(8,128)S(1)}, f32[16,16]{1,0:T(8,128)S(1)}) all-reduce(f32[16,16]{1,0:T(8,128)S(1)} %fusion.192, f32[16,16]{1,0:T(8,128)S(1)} %fusion.191, f32[16,16]{1,0:T(8,128)S(1)} %fusion.193), channel_id=1, replica_groups=mesh['wide'=8,'narrow'=4] {'wide'}, use_global_device_ids=true, to_apply=%region_7.10 | all-reduce | flops 768 | bytes 6144 | tf_op jit(solution)/shard_map/psum | solution.py:76
  248.2 4.1 all-to-all-start.4
  253.8 8.8 %all-to-all-done.4 = f32[8,8,16,128]{3,2,1,0:T(8,128)} async-done(((f32[8,8,16,128]{3,2,1,0:T(8,128)}), f32[8,8,16,128]{3,2,1,0:T(8,128)}, u32[]{:S(2)}, u32[]{:S(2)}) %all-to-all-start.4) | async-done | bytes 524320 | tf_op jit(solution)/shard_map/all_to_all | solution.py:87
  264.2 25.6 %while.43 = (s32[]{:T(128)}, f32[2,32,16,128]{3,2,1,0:T(8,128)}, f32[2,32,16,128]{3,2,1,0:T(8,128)}, f32[2,32,16,128]{3,2,1,0:T(8,128)}, s32[2,32]{1,0:T(2,128)S...) while((s32[]{:T(128)}, f32[2,32,16,128]{3,2,1,0:T(8,128)}, ...), condition=%wide.region_10.13_spmd, body=%wide.region_9.12_spmd.sunk | while | flops 471860320 | bytes 17833084 | solution.py:91
  269.2 5.1 %fusion.276 = f32[2,32,16,128]{3,2,1,0:T(8,128)} fusion(f32[2,32,16,128]{3,2,1,0:T(8,128)} %get-tuple-element.571, s32[]{:T(128)} %get-tuple-element.570, f32[32,128,128]{2,1,0:T(8,128)S(1)} %fusion.275, f32[2,32,16,128]{3,2,1,0:T(8,128)} %get-tuple-element.582), kind=kOutput, calls=%fused_computation.47.clone.1 | convolution fusion | flops 101711872 | bytes 2622464 | tf_op jit(solution)/shard_map/while/body/eval_jaxpr/pab,prb->pra/dot_general | solution.py:39
  282.0 5.1 %fusion.276 = f32[2,32,16,128]{3,2,1,0:T(8,128)} fusion(f32[2,32,16,128]{3,2,1,0:T(8,128)} %get-tuple-element.571, s32[]{:T(128)} %get-tuple-element.570, f32[32,128,128]{2,1,0:T(8,128)S(1)} %fusion.275, f32[2,32,16,128]{3,2,1,0:T(8,128)} %get-tuple-element.582), kind=kOutput, calls=%fused_computation.47.clone.1 | convolution fusion | flops 101711872 | bytes 2622464 | tf_op jit(solution)/shard_map/while/body/eval_jaxpr/pab,prb->pra/dot_general | solution.py:39
  291.7 3.7 all-to-all-start.5
  297.4 8.3 %all-to-all-done.5 = f32[8,8,2048]{2,1,0:T(8,128)S(1)} async-done(((f32[8,8,2048]{2,1,0:T(8,128)}), f32[8,8,2048]{2,1,0:T(8,128)S(1)}, u32[]{:S(2)}, u32[]{:S(2)}) %all-to-all-start.5) | async-done | bytes 524320 | tf_op jit(solution)/shard_map/all_to_all | solution.py:96
  310.9 6.4 %collective-permute-done.3 = f32[32,2048]{1,0:T(8,128)S(1)} collective-permute-done((f32[32,2048]{1,0:T(8,128)S(1)}, f32[32,2048]{1,0:T(8,128)S(1)}, u32[]{:S(2)}, u32[]{:S(2)}) %collective-permute-start.3) | collective-permute-done | bytes 262176 | tf_op jit(solution)/shard_map/ppermute | solution.py:22
  319.3 35.3 %all-reduce.1 = (f32[16,16]{1,0:T(8,128)S(1)}, f32[16,16]{1,0:T(8,128)S(1)}, f32[16,16]{1,0:T(8,128)S(1)}) all-reduce(f32[16,16]{1,0:T(8,128)S(1)} %fusion.195, f32[16,16]{1,0:T(8,128)S(1)} %fusion.194, f32[16,16]{1,0:T(8,128)S(1)} %fusion.196), channel_id=1, replica_groups=mesh['wide'=8,'narrow'=4] {'wide'}, use_global_device_ids=true, to_apply=%region_12.15 | all-reduce | flops 768 | bytes 6144 | tf_op jit(solution)/shard_map/psum | solution.py:76
  361.6 4.4 all-to-all-start.6
  367.4 8.6 %all-to-all-done.6 = f32[8,8,16,128]{3,2,1,0:T(8,128)} async-done(((f32[8,8,16,128]{3,2,1,0:T(8,128)}), f32[8,8,16,128]{3,2,1,0:T(8,128)}, u32[]{:S(2)}, u32[]{:S(2)}) %all-to-all-start.6) | async-done | bytes 524320 | tf_op jit(solution)/shard_map/all_to_all | solution.py:87
  377.7 25.6 %while.44 = (s32[]{:T(128)}, f32[2,32,16,128]{3,2,1,0:T(8,128)}, f32[2,32,16,128]{3,2,1,0:T(8,128)}, f32[2,32,16,128]{3,2,1,0:T(8,128)}, s32[2,32]{1,0:T(2,128)S...) while((s32[]{:T(128)}, f32[2,32,16,128]{3,2,1,0:T(8,128)}, ...), condition=%wide.region_15.18_spmd, body=%wide.region_14.17_spmd.sunk | while | flops 471860320 | bytes 17833084 | solution.py:91
  382.7 5.1 %fusion.284 = f32[2,32,16,128]{3,2,1,0:T(8,128)} fusion(f32[2,32,16,128]{3,2,1,0:T(8,128)} %get-tuple-element.598, s32[]{:T(128)} %get-tuple-element.597, f32[32,128,128]{2,1,0:T(8,128)S(1)} %fusion.283, f32[2,32,16,128]{3,2,1,0:T(8,128)} %get-tuple-element.609), kind=kOutput, calls=%fused_computation.77.clone.1 | convolution fusion | flops 101711872 | bytes 2622464 | tf_op jit(solution)/shard_map/while/body/eval_jaxpr/pab,prb->pra/dot_general | solution.py:39
  392.5 2.9 fusion.283
  395.5 5.1 %fusion.284 = f32[2,32,16,128]{3,2,1,0:T(8,128)} fusion(f32[2,32,16,128]{3,2,1,0:T(8,128)} %get-tuple-element.598, s32[]{:T(128)} %get-tuple-element.597, f32[32,128,128]{2,1,0:T(8,128)S(1)} %fusion.283, f32[2,32,16,128]{3,2,1,0:T(8,128)} %get-tuple-element.609), kind=kOutput, calls=%fused_computation.77.clone.1 | convolution fusion | flops 101711872 | bytes 2622464 | tf_op jit(solution)/shard_map/while/body/eval_jaxpr/pab,prb->pra/dot_general | solution.py:39
  405.2 3.7 all-to-all-start.7
  410.1 9.1 %all-to-all-done.7 = f32[8,8,2048]{2,1,0:T(8,128)S(1)} async-done(((f32[8,8,2048]{2,1,0:T(8,128)}), f32[8,8,2048]{2,1,0:T(8,128)S(1)}, u32[]{:S(2)}, u32[]{:S(2)}) %all-to-all-start.7) | async-done | bytes 524320 | tf_op jit(solution)/shard_map/all_to_all | solution.py:96
  423.3 6.3 %collective-permute-done.5 = f32[32,2048]{1,0:T(8,128)S(1)} collective-permute-done((f32[32,2048]{1,0:T(8,128)S(1)}, f32[32,2048]{1,0:T(8,128)S(1)}, u32[]{:S(2)}, u32[]{:S(2)}) %collective-permute-start.5) | collective-permute-done | bytes 262176 | tf_op jit(solution)/shard_map/ppermute | solution.py:22
  431.8 35.3 %all-reduce = (f32[16,16]{1,0:T(8,128)S(1)}, f32[16,16]{1,0:T(8,128)S(1)}, f32[16,16]{1,0:T(8,128)S(1)}) all-reduce(f32[16,16]{1,0:T(8,128)S(1)} %fusion.198, f32[16,16]{1,0:T(8,128)S(1)} %fusion.197, f32[16,16]{1,0:T(8,128)S(1)} %fusion.199), channel_id=1, replica_groups=mesh['wide'=8,'narrow'=4] {'wide'}, use_global_device_ids=true, to_apply=%region_17.20 | all-reduce | flops 768 | bytes 6144 | tf_op jit(solution)/shard_map/psum | solution.py:76
  (169 shorter events, 119.7 us)
Async XLA Ops:
  0.6 8.8 %copy-start = (f32[16,4096]{1,0:T(8,128)S(1)}, f32[16,4096]{1,0:T(8,128)}, u32[]{:S(2)}) copy-start(f32[16,4096]{1,0:T(8,128)} %param.13) | copy-start | bytes 786436
  2.1 36.7 %all-to-all-start = ((s32[8,1,8]{2,1,0:T(1,128)}), s32[8,1,8]{2,1,0:T(1,128)S(1)}, u32[]{:S(2)}, u32[]{:S(2)}) async-start(s32[8,1,8]{2,1,0:T(1,128)} %bitcast.22), calls=%async_computation | async-start | bytes 8192 | tf_op jit(solution)/shard_map/all_to_all | solution.py:57
  40.4 13.8 %all-to-all-start.1 = ((f32[8,8,16,128]{3,2,1,0:T(8,128)}), f32[8,8,16,128]{3,2,1,0:T(8,128)S(1)}, u32[]{:S(2)}, u32[]{:S(2)}) async-start(f32[8,8,16,128]{3,2,1,0:T(8,128)} %bitcast.29), calls=%async_computation.1 | async-start | bytes 1048576 | tf_op jit(solution)/shard_map/all_to_all | solution.py:87
  54.2 4.7 copy-start.4
  54.2 93.5 %all-to-all-start.2 = ((bf16[8,8,128,256]{3,2,1,0:T(8,128)(2,1)}), bf16[8,8,128,256]{3,2,1,0:T(8,128)(2,1)}, u32[]{:S(2)}, u32[]{:S(2)}) async-start(bf16[8,8,128,256]{3,2,1,0:T(8,128)(2,1)} %bitcast.309), calls=%async_computation.2 | async-start | bytes 8388608 | tf_op jit(solution)/shard_map/all_to_all | solution.py:60
  154.3 4.1 copy-start.2
  166.1 4.1 copy-start.2
  174.9 18.2 %all-to-all-start.3 = ((f32[8,8,2048]{2,1,0:T(8,128)}), f32[8,8,2048]{2,1,0:T(8,128)S(1)}, u32[]{:S(2)}, u32[]{:S(2)}) async-start(f32[8,8,2048]{2,1,0:T(8,128)} %reshape.254), calls=%async_computation.3 | async-start | bytes 1048576 | tf_op jit(solution)/shard_map/all_to_all | solution.py:96
  194.6 1.6 collective-permute-start
  196.2 8.4 %collective-permute-start.1 = (f32[32,2048]{1,0:T(8,128)S(1)}, f32[32,2048]{1,0:T(8,128)S(1)}, u32[]{:S(2)}, u32[]{:S(2)}) collective-permute-start(f32[32,2048]{1,0:T(8,128)S(1)} %add.164), channel_id=1, source_target_pairs={{0,2},{1,3},{2,0},{3,1},{4,6},{5,7},{6,4},{7,5},{8,10},{9,11},{10,... | collective-permute-start | bytes 786440 | tf_op jit(solution)/shard_map/ppermute | solution.py:22
  248.2 14.4 %all-to-all-start.4 = ((f32[8,8,16,128]{3,2,1,0:T(8,128)}), f32[8,8,16,128]{3,2,1,0:T(8,128)}, u32[]{:S(2)}, u32[]{:S(2)}) async-start(f32[8,8,16,128]{3,2,1,0:T(8,128)} %bitcast.321), calls=%async_computation.4 | async-start | bytes 1048576 | tf_op jit(solution)/shard_map/all_to_all | solution.py:87
  269.2 5.1 %copy-start.3 = (f32[2,32,16,128]{3,2,1,0:T(8,128)S(1)}, f32[2,32,16,128]{3,2,1,0:T(8,128)}, u32[]{:S(2)}) copy-start(f32[2,32,16,128]{3,2,1,0:T(8,128)} %get-tuple-element.586) | copy-start | bytes 1572868 | tf_op jit(solution)/shard_map/while
  282.0 5.1 %copy-start.3 = (f32[2,32,16,128]{3,2,1,0:T(8,128)S(1)}, f32[2,32,16,128]{3,2,1,0:T(8,128)}, u32[]{:S(2)}) copy-start(f32[2,32,16,128]{3,2,1,0:T(8,128)} %get-tuple-element.586) | copy-start | bytes 1572868 | tf_op jit(solution)/shard_map/while
  291.7 14.0 %all-to-all-start.5 = ((f32[8,8,2048]{2,1,0:T(8,128)}), f32[8,8,2048]{2,1,0:T(8,128)S(1)}, u32[]{:S(2)}, u32[]{:S(2)}) async-start(f32[8,8,2048]{2,1,0:T(8,128)} %reshape.261), calls=%async_computation.5 | async-start | bytes 1048576 | tf_op jit(solution)/shard_map/all_to_all | solution.py:96
  307.2 1.6 collective-permute-start.2
  308.8 8.4 %collective-permute-start.3 = (f32[32,2048]{1,0:T(8,128)S(1)}, f32[32,2048]{1,0:T(8,128)S(1)}, u32[]{:S(2)}, u32[]{:S(2)}) collective-permute-start(f32[32,2048]{1,0:T(8,128)S(1)} %add.167), channel_id=1, source_target_pairs={{0,2},{1,3},{2,0},{3,1},{4,6},{5,7},{6,4},{7,5},{8,10},{9,11},{10,... | collective-permute-start | bytes 786440 | tf_op jit(solution)/shard_map/ppermute | solution.py:22
  361.6 14.4 %all-to-all-start.6 = ((f32[8,8,16,128]{3,2,1,0:T(8,128)}), f32[8,8,16,128]{3,2,1,0:T(8,128)}, u32[]{:S(2)}, u32[]{:S(2)}) async-start(f32[8,8,16,128]{3,2,1,0:T(8,128)} %bitcast.320), calls=%async_computation.6 | async-start | bytes 1048576 | tf_op jit(solution)/shard_map/all_to_all | solution.py:87
  382.7 5.1 %copy-start.1 = (f32[2,32,16,128]{3,2,1,0:T(8,128)S(1)}, f32[2,32,16,128]{3,2,1,0:T(8,128)}, u32[]{:S(2)}) copy-start(f32[2,32,16,128]{3,2,1,0:T(8,128)} %get-tuple-element.613) | copy-start | bytes 1572868 | tf_op jit(solution)/shard_map/while
  395.5 5.1 %copy-start.1 = (f32[2,32,16,128]{3,2,1,0:T(8,128)S(1)}, f32[2,32,16,128]{3,2,1,0:T(8,128)}, u32[]{:S(2)}) copy-start(f32[2,32,16,128]{3,2,1,0:T(8,128)} %get-tuple-element.613) | copy-start | bytes 1572868 | tf_op jit(solution)/shard_map/while
  405.2 13.9 %all-to-all-start.7 = ((f32[8,8,2048]{2,1,0:T(8,128)}), f32[8,8,2048]{2,1,0:T(8,128)S(1)}, u32[]{:S(2)}, u32[]{:S(2)}) async-start(f32[8,8,2048]{2,1,0:T(8,128)} %reshape.268), calls=%async_computation.7 | async-start | bytes 1048576 | tf_op jit(solution)/shard_map/all_to_all | solution.py:96
  419.6 1.6 collective-permute-start.4
  421.3 8.4 %collective-permute-start.5 = (f32[32,2048]{1,0:T(8,128)S(1)}, f32[32,2048]{1,0:T(8,128)S(1)}, u32[]{:S(2)}, u32[]{:S(2)}) collective-permute-start(f32[32,2048]{1,0:T(8,128)S(1)} %add.170), channel_id=1, source_target_pairs={{0,2},{1,3},{2,0},{3,1},{4,6},{5,7},{6,4},{7,5},{8,10},{9,11},{10,... | collective-permute-start | bytes 786440 | tf_op jit(solution)/shard_map/ppermute | solution.py:22
